TPU v7x, 256 devices: a whole 4x4x8 slice. The times are simulated.
256 devices in a mesh: row: 8 (over y, core), col: 32 (over x, z).
Axes of the slice: x: 4, y: 4, z: 8, core: 2. Of those that a mesh axis runs over, the one named last changes fastest.
Arguments:
- stored: float32 [20, 8, 128, 5, 32, 128], P(None, 'row', None, None, 'col'), may hold values from -1 to 13
- rhs: float32 [5, 32, 128, 128], P(None, 'col'), may hold values from -60 to 60
Outputs:
- solution: float32 [5, 32, 128, 128], P(None, 'col')
- residual: float32 [5, 32, 128, 128], P(None, 'col')
All inputs are finite; a program needn't handle non-finite values.
Results may differ from a plain program's by a relative error of at most 0.0003.
Values sent between devices are 32-bit elements; how exact they have to be, the bound alone decides.
A program may use at most 128 MiB of HBM per device.

v0:
```python
import jax
import jax.numpy as jnp
from jax import lax
from jax.sharding import PartitionSpec as P

ITERS = 2


HIGHEST = lax.Precision.HIGHEST


def partner_2(value, axis, distance):
    mask = 2**distance
    pairs = [(source, source ^ mask) for source in range(lax.axis_size(axis))]
    return lax.ppermute(value, axis, pairs)


def spread(value, axis, source):
    kept = jnp.where(lax.axis_index(axis) == source, value, 0).astype(value.dtype)
    return lax.psum(kept, axis)


def gram_local(left_side, right_side):
    columns_n = left_side.shape[-1]
    return jnp.einsum(
        "nk,nl->kl",
        left_side.reshape(-1, columns_n),
        right_side.reshape(-1, columns_n),
        precision=HIGHEST,
        preferred_element_type=jnp.float32,
    )


def mix_right(vectors, matrix):
    columns_n = vectors.shape[-1]
    return jnp.dot(
        vectors.reshape(-1, columns_n),
        matrix,
        precision=HIGHEST,
        preferred_element_type=jnp.float32,
    ).reshape(vectors.shape)


def solve_spd(matrix, target):
    factor = jnp.linalg.cholesky(matrix)
    return jax.scipy.linalg.cho_solve((factor, True), target)


def to_rowset(column_set, row_index, col_index):
    low_bits = lax.axis_size("row").bit_length() - 1
    high_bits = lax.axis_size("col").bit_length() - 1
    current = column_set
    for bit_pos in range(low_bits):
        partner = partner_2(current, "col", bit_pos)
        differs = col_index >> bit_pos & 1 != row_index >> bit_pos & 1
        current = jnp.where(differs, partner, current)
    joined = current[:, None]
    for bit_pos in range(low_bits, high_bits):
        partner = partner_2(joined, "col", bit_pos)
        lower_half = col_index >> bit_pos & 1 == 0
        joined = jnp.where(
            lower_half,
            jnp.concatenate([joined, partner], axis=1),
            jnp.concatenate([partner, joined], axis=1),
        )
    return joined.reshape((-1,) + column_set.shape[1:])


def to_colset(row_set, col_index):
    rows_n = lax.axis_size("row")
    groups = lax.axis_size("col") // rows_n
    shape_in = row_set.shape
    regrouped = row_set.reshape(shape_in[:-3] + (shape_in[-3] // groups, groups) + shape_in[-2:])
    selected = lax.dynamic_index_in_dim(
        regrouped, col_index // rows_n, regrouped.ndim - 3, keepdims=False
    )
    return spread(selected, "row", col_index % rows_n)


def local_products(lower_part, column_set, row_set):
    columns_n = column_set.shape[-1]
    by_rows = jnp.dot(
        lower_part,
        column_set.reshape(-1, columns_n),
        precision=HIGHEST,
        preferred_element_type=jnp.float32,
    )
    by_columns = jnp.einsum(
        "nm,nk->mk",
        lower_part,
        row_set.reshape(-1, columns_n),
        precision=HIGHEST,
        preferred_element_type=jnp.float32,
    )
    return (by_rows, by_columns)


def columns_whole(by_columns, shape_out):
    return lax.psum(by_columns, "row").reshape(shape_out)


def rows_whole(by_rows, shape_out):
    return lax.psum(by_rows, "col").reshape(shape_out)


def per_device(stored, rhs):
    row_index = lax.axis_index("row")
    col_index = lax.axis_index("col")
    rows_n = lax.axis_size("row")
    cols_n = lax.axis_size("col")
    row_blocks = stored.shape[0]
    block_size = stored.shape[2]
    col_blocks = stored.shape[3]
    columns_n = rhs.shape[-1]
    block_rows = jnp.arange(row_blocks, dtype=jnp.int32) * rows_n + row_index
    block_cols = jnp.arange(col_blocks, dtype=jnp.int32) * cols_n + col_index
    weight = jnp.where(
        block_rows[:, None] > block_cols[None, :],
        1.0,
        jnp.where(block_rows[:, None] == block_cols[None, :], 0.5, 0.0),
    ).astype(jnp.float32)
    lower_part = (
        stored.reshape(row_blocks, block_size, col_blocks, block_size) * weight[:, None, :, None]
    ).reshape(row_blocks * block_size, col_blocks * block_size)
    start_set = rhs.reshape(col_blocks, block_size, columns_n)

    def reduce_grams(stacked):
        return lax.psum(stacked, "row")

    vectors = to_rowset(start_set, row_index, col_index)
    solution = jnp.zeros_like(vectors)
    residual = vectors
    direction = vectors
    gram_now = reduce_grams(gram_local(residual, residual)[None])[0]
    for iteration in range(ITERS):
        column_set = to_colset(direction, col_index)
        by_rows, by_columns = local_products(lower_part, column_set, direction)
        row_part = rows_whole(by_rows, direction.shape)
        applied = row_part + to_rowset(
            columns_whole(by_columns, column_set.shape), row_index, col_index
        )
        last_turn = iteration + 1 == ITERS
        gram_sums = reduce_grams(gram_local(direction, applied)[None])
        curvature = gram_sums[0]
        step_size = solve_spd(curvature, gram_now)
        solution = solution + mix_right(direction, step_size)
        residual = residual - mix_right(applied, step_size)
        if not last_turn:
            gram_next = reduce_grams(gram_local(residual, residual)[None])[0]
            mix_factor = solve_spd(gram_now, gram_next)
            direction = residual + mix_right(direction, mix_factor)
            gram_now = gram_next
    both_sets = to_colset(jnp.stack([solution, residual]), col_index)
    final_pair = (both_sets[0], both_sets[1])
    return (final_pair[0].reshape(rhs.shape), final_pair[1].reshape(rhs.shape))


def solution(mesh):
    placed = (P(None, "row", None, None, "col", None), P(None, "col", None, None))
    return jax.shard_map(
        per_device,
        mesh=mesh,
        in_specs=placed,
        out_specs=(P(None, "col", None, None), P(None, "col", None, None)),
        check_vma=False,
    )
```

profile of v0, /device:TPU:1, one launch (start us, length us, event | category | flops | bytes accessed | tf_op | source)
XLA Modules:
  0.0 994.5 jit_solution(8550308270842308896)
XLA Ops:
  7.2 2.6 collective-permute-start
  9.8 6.7 collective-permute-done
  17.5 3.9 collective-permute-start.1
  21.4 14.1 %collective-permute-done.1 = f32[5,128,128]{2,1,0:T(8,128)S(1)} collective-permute-done((f32[5,128,128]{2,1,0:T(8,128)S(1)}, f32[5,128,128]{2,1,0:T(8,128)S(1)}, u32[]{:S(2)}, u32[]{:S(2)}) %collective-permute-start.1) | collective-permute-done | bytes 327712 | tf_op jit(solution)/shard_map/ppermute | solution.py:15
  35.6 6.5 collective-permute-start.2
  42.1 13.0 %collective-permute-done.2 = f32[5,128,128]{2,1,0:T(8,128)S(1)} collective-permute-done((f32[5,128,128]{2,1,0:T(8,128)S(1)}, f32[5,128,128]{2,1,0:T(8,128)S(1)}, u32[]{:S(2)}, u32[]{:S(2)}) %collective-permute-start.2) | collective-permute-done | bytes 327712 | tf_op jit(solution)/shard_map/ppermute | solution.py:15
  55.1 1.3 collective-permute-start.3
  56.5 5.1 collective-permute-done.3
  61.7 2.8 collective-permute-start.4
  64.5 23.9 %multiply_reduce_fusion = f32[20,128,5,128]{3,2,1,0:T(8,128)} fusion(f32[20,1,128,5,1,128]{5,4,3,2,1,0:T(1,128)} %param.5, f32[20,5]{1,0:T(8,128)S(1)} %select_select_fusion.3), kind=kLoop, calls=%fused_computation.8 | loop fusion | flops 1638400 | bytes 13107600 | tf_op jit(solution)/shard_map/mul | solution.py:123
  89.3 14.6 %fusion.4 = f32[640,128]{1,0:T(8,128)} fusion(f32[2560,128]{1,0:T(8,128)S(1)} %bitcast.127, f32[320,8,5,128]{3,2,1,0:T(8,128)} %bitcast.123), kind=kOutput, calls=%fused_computation.4 | convolution fusion | flops 2516582400 | bytes 8192000 | tf_op jit(solution)/shard_map/nm,nk->mk/dot_general | solution.py:88
  103.9 66.9 %all-reduce.26.cloned.1.call-done = (f32[640,128]{1,0:T(8,128)}, f32[5,128,128]{2,1,0:T(8,128)}) async-done(((f32[640,128]{1,0:T(8,128)}, f32[5,128,128]{2,1,0:T(8,128)}), (f32[640,128]{1,0:T(8,128)}, f32[5,128,128]{2,1,0:T(8,128)})) %all-reduce.26.cloned.1.call-update) | async-done | bytes 655376 | tf_op jit(solution)/shard_map/psum | solution.py:20
  170.8 1.3 collective-permute-start.5
  172.1 5.5 collective-permute-done.5
  177.6 2.6 collective-permute-start.6
  180.1 13.3 %collective-permute-done.6 = f32[5,128,128]{2,1,0:T(8,128)S(1)} collective-permute-done((f32[5,128,128]{2,1,0:T(8,128)S(1)}, f32[5,128,128]{2,1,0:T(8,128)S(1)}, u32[]{:S(2)}, u32[]{:S(2)}) %collective-permute-start.6) | collective-permute-done | bytes 327712 | tf_op jit(solution)/shard_map/ppermute | solution.py:15
  193.4 6.4 collective-permute-start.7
  199.9 10.1 %fusion.6 = f32[2560,128]{1,0:T(8,128)} fusion(f32[640,128]{1,0:T(8,128)S(1)} %copy-done.5, f32[320,8,5,128]{3,2,1,0:T(8,128)} %bitcast.124), kind=kOutput, calls=%fused_computation.6 | convolution fusion | flops 2516582400 | bytes 8192000 | tf_op jit(solution)/shard_map/dot_general | solution.py:82
  210.1 2.0 collective-permute-done.7
  212.1 1.3 collective-permute-start.8
  213.4 4.7 collective-permute-done.8
  218.1 2.8 collective-permute-start.9
  220.9 2.9 convolution_bitcast_fusion.5
  223.8 15.3 %collective-permute-done.9 = f32[5,2,128,128]{3,2,0,1:T(8,128)S(1)} collective-permute-done((f32[5,2,128,128]{3,2,0,1:T(8,128)S(1)}, f32[5,2,128,128]{3,2,0,1:T(8,128)S(1)}, u32[]{:S(2)}, u32[]{:S(2)}) %collective-permute-start.9) | collective-permute-done | bytes 655392 | tf_op jit(solution)/shard_map/ppermute | solution.py:15
  239.2 1.1 copy.22
  240.4 124.4 %all-reduce.12.cloned.1.call-done = f32[2560,128]{1,0:T(8,128)} async-done(((f32[2560,128]{1,0:T(8,128)}), f32[2560,128]{1,0:T(8,128)}) %all-reduce.12.cloned.1.call-update) | async-done | bytes 1310736 | tf_op jit(solution)/shard_map/psum | solution.py:103
  364.8 1.8 bitcast_add_fusion.2
  366.7 2.9 fusion.31
  370.0 64.0 %all-reduce.24.cloned.1.call-done = (f32[128,128]{0,1:T(8,128)}, f32[128,128]{0,1:T(8,128)}) async-done(((f32[128,128]{0,1:T(8,128)}, f32[128,128]{0,1:T(8,128)}), (f32[128,128]{0,1:T(8,128)}, f32[128,128]{0,1:T(8,128)})) %all-reduce.24.cloned.1.call-update) | async-done | bytes 131088 | tf_op jit(solution)/shard_map/psum | solution.py:128
  436.7 11.7 %cholesky.70 = f32[128,128]{1,0:T(8,128)S(1)} custom-call(f32[128,128]{1,0:T(8,128)S(1)} %get-tuple-element.12), custom_call_target="Cholesky" | custom-call | tf_op jit(solution)/shard_map/jit(cholesky)/cholesky | solution.py:45
  449.1 11.7 %cholesky.59 = f32[128,128]{1,0:T(8,128)S(1)} custom-call(f32[128,128]{1,0:T(8,128)S(1)} %get-tuple-element.13), custom_call_target="Cholesky" | custom-call | tf_op jit(solution)/shard_map/jit(cholesky)/cholesky | solution.py:45
  462.2 9.8 custom-call.9
  472.0 1.1 fusion.24
  473.3 2.5 convolution_subtract_fusion.1
  475.8 3.0 convolution_bitcast_fusion.4
  479.6 9.8 custom-call.10
  489.4 52.6 %all-reduce.14.cloned.1.call-done = f32[128,128]{1,0:T(8,128)} async-done(((f32[128,128]{1,0:T(8,128)}), f32[128,128]{1,0:T(8,128)}) %all-reduce.14.cloned.1.call-update) | async-done | bytes 65552 | tf_op jit(solution)/shard_map/psum | solution.py:128
  543.3 1.2 convolution_add_fusion
  545.4 14.6 %fusion = f32[640,128]{1,0:T(8,128)} fusion(f32[2560,128]{1,0:T(8,128)S(1)} %bitcast.133, f32[320,8,5,128]{3,2,1,0:T(8,128)} %bitcast.125), kind=kOutput, calls=%fused_computation | convolution fusion | flops 2516582400 | bytes 8192000 | tf_op jit(solution)/shard_map/nm,nk->mk/dot_general | solution.py:88
  560.0 65.8 %all-reduce.22.cloned.1.call-done = (f32[640,128]{1,0:T(8,128)}, f32[5,128,128]{2,1,0:T(8,128)}) async-done(((f32[640,128]{1,0:T(8,128)}, f32[5,128,128]{2,1,0:T(8,128)}), (f32[640,128]{1,0:T(8,128)}, f32[5,128,128]{2,1,0:T(8,128)})) %all-reduce.22.cloned.1.call-update) | async-done | bytes 655376 | tf_op jit(solution)/shard_map/psum | solution.py:20
  625.8 1.3 collective-permute-start.10
  627.1 5.5 collective-permute-done.10
  632.6 2.6 collective-permute-start.11
  635.1 13.3 %collective-permute-done.11 = f32[5,128,128]{2,1,0:T(8,128)S(1)} collective-permute-done((f32[5,128,128]{2,1,0:T(8,128)S(1)}, f32[5,128,128]{2,1,0:T(8,128)S(1)}, u32[]{:S(2)}, u32[]{:S(2)}) %collective-permute-start.11) | collective-permute-done | bytes 327712 | tf_op jit(solution)/shard_map/ppermute | solution.py:15
  648.4 6.4 collective-permute-start.12
  654.9 10.1 %fusion.2 = f32[2560,128]{1,0:T(8,128)} fusion(f32[640,128]{1,0:T(8,128)S(1)} %copy-done.4, f32[320,8,5,128]{3,2,1,0:T(8,128)} %bitcast.126), kind=kOutput, calls=%fused_computation.2 | convolution fusion | flops 2516582400 | bytes 8192000 | tf_op jit(solution)/shard_map/dot_general | solution.py:82
  665.1 2.0 collective-permute-done.12
  667.1 1.3 collective-permute-start.13
  668.4 4.7 collective-permute-done.13
  673.1 2.8 collective-permute-start.14
  675.9 18.2 %collective-permute-done.14 = f32[5,2,128,128]{3,2,0,1:T(8,128)S(1)} collective-permute-done((f32[5,2,128,128]{3,2,0,1:T(8,128)S(1)}, f32[5,2,128,128]{3,2,0,1:T(8,128)S(1)}, u32[]{:S(2)}, u32[]{:S(2)}) %collective-permute-start.14) | collective-permute-done | bytes 655392 | tf_op jit(solution)/shard_map/ppermute | solution.py:15
  694.2 1.2 copy.29
  695.4 124.4 %all-reduce.16.cloned.1.call-done = f32[2560,128]{1,0:T(8,128)} async-done(((f32[2560,128]{1,0:T(8,128)}), f32[2560,128]{1,0:T(8,128)}) %all-reduce.16.cloned.1.call-update) | async-done | bytes 1310736 | tf_op jit(solution)/shard_map/psum | solution.py:103
  819.8 2.0 bitcast_add_fusion.1
  821.9 2.9 convolution_bitcast_fusion.3
  825.2 2.9 bitcast_add_fusion
  828.1 60.5 %all-reduce.18.cloned.1.call-done = f32[128,128]{0,1:T(8,128)} async-done(((f32[128,128]{0,1:T(8,128)}), f32[128,128]{0,1:T(8,128)}) %all-reduce.18.cloned.1.call-update) | async-done | bytes 65552 | tf_op jit(solution)/shard_map/psum | solution.py:128
  890.4 11.7 %cholesky.81 = f32[128,128]{1,0:T(8,128)S(1)} custom-call(f32[128,128]{1,0:T(8,128)S(1)} %fusion.18), custom_call_target="Cholesky" | custom-call | tf_op jit(solution)/shard_map/jit(cholesky)/cholesky | solution.py:45
  903.4 9.8 custom-call.11
  913.8 2.6 fusion.32
  916.4 1.2 convolution_subtract_fusion
  917.6 1.2 convolution_add_fusion.1
  919.7 65.6 %all-reduce.20.cloned.1.call-done = f32[2,5,128,128]{3,2,1,0:T(8,128)} async-done(((f32[2,5,128,128]{3,2,1,0:T(8,128)}), f32[2,5,128,128]{3,2,1,0:T(8,128)}) %all-reduce.20.cloned.1.call-update) | async-done | bytes 655376 | tf_op jit(solution)/shard_map/psum | solution.py:20
  985.3 2.0 slice_bitcast_fusion
  (71 shorter events, 16.2 us)
Async XLA Ops:
  7.2 163.6 %all-reduce.26.cloned.1.call-start = ((), (), s32[]{:S(2)}) async-start(), calls=%async_computation.7 | async-start | bytes 1310720 | tf_op jit(solution)/shard_map/psum | solution.py:20
  7.2 9.2 collective-permute-start
  17.5 18.1 %collective-permute-start.1 = (f32[5,128,128]{2,1,0:T(8,128)S(1)}, f32[5,128,128]{2,1,0:T(8,128)S(1)}, u32[]{:S(2)}, u32[]{:S(2)}) collective-permute-start(f32[5,128,128]{2,1,0:T(8,128)S(1)} %broadcast_select_fusion.2), channel_id=1, source_target_pairs={{0,2},{1,3},{2,0},{3,1},{4,6},{5,7},{6,4},{7,5},{8,10},{9,11},{10,... | collective-permute-start | bytes 983048 | tf_op jit(solution)/shard_map/ppermute | solution.py:15
  35.6 19.5 %collective-permute-start.2 = (f32[5,128,128]{2,1,0:T(8,128)S(1)}, f32[5,128,128]{2,1,0:T(8,128)S(1)}, u32[]{:S(2)}, u32[]{:S(2)}) collective-permute-start(f32[5,128,128]{2,1,0:T(8,128)S(1)} %broadcast_select_fusion.5), channel_id=1, source_target_pairs={{0,4},{1,5},{2,6},{3,7},{4,0},{5,1},{6,2},{7,3},{8,12},{9,13},{10,... | collective-permute-start | bytes 983048 | tf_op jit(solution)/shard_map/ppermute | solution.py:15
  55.1 6.5 collective-permute-start.3
  61.7 26.7 %collective-permute-start.4 = (f32[5,2,128,128]{3,2,1,0:T(8,128)S(1)}, f32[5,2,128,128]{3,2,1,0:T(8,128)S(1)}, u32[]{:S(2)}, u32[]{:S(2)}) collective-permute-start(f32[5,2,128,128]{3,2,1,0:T(8,128)S(1)} %maximum_select_fusion.3), channel_id=1, source_target_pairs={{0,16},{1,17},{2,18},{3,19},{4,20},{5,21},{6,22},{7,23},{8,24},{9,... | collective-permute-start | bytes 1966088 | tf_op jit(solution)/shard_map/ppermute | solution.py:15
  103.9 260.9 %all-reduce.12.cloned.1.call-start = ((), (), s32[]{:S(2)}) async-start(), calls=%async_computation | async-start | bytes 2621440 | tf_op jit(solution)/shard_map/psum | solution.py:103
  170.8 29.1 %copy-start.5 = (f32[640,128]{1,0:T(8,128)S(1)}, f32[640,128]{1,0:T(8,128)}, u32[]{:S(2)}) copy-start(f32[640,128]{1,0:T(8,128)} %get-tuple-element.8) | copy-start | bytes 983044
  170.8 6.7 collective-permute-start.5
  177.6 15.8 %collective-permute-start.6 = (f32[5,128,128]{2,1,0:T(8,128)S(1)}, f32[5,128,128]{2,1,0:T(8,128)S(1)}, u32[]{:S(2)}, u32[]{:S(2)}) collective-permute-start(f32[5,128,128]{2,1,0:T(8,128)S(1)} %broadcast_select_fusion.1), channel_id=1, source_target_pairs={{0,2},{1,3},{2,0},{3,1},{4,6},{5,7},{6,4},{7,5},{8,10},{9,11},{10,... | collective-permute-start | bytes 983048 | tf_op jit(solution)/shard_map/ppermute | solution.py:15
  193.4 18.6 %collective-permute-start.7 = (f32[5,128,128]{2,1,0:T(8,128)S(1)}, f32[5,128,128]{2,1,0:T(8,128)S(1)}, u32[]{:S(2)}, u32[]{:S(2)}) collective-permute-start(f32[5,128,128]{2,1,0:T(8,128)S(1)} %broadcast_select_fusion.4), channel_id=1, source_target_pairs={{0,4},{1,5},{2,6},{3,7},{4,0},{5,1},{6,2},{7,3},{8,12},{9,13},{10,... | collective-permute-start | bytes 983048 | tf_op jit(solution)/shard_map/ppermute | solution.py:15
  210.0 223.9 %all-reduce.24.cloned.1.call-start = ((), (), s32[]{:S(2)}) async-start(), calls=%async_computation.6 | async-start | bytes 262144 | tf_op jit(solution)/shard_map/psum | solution.py:128
  212.1 6.0 collective-permute-start.8
  218.1 21.0 %collective-permute-start.9 = (f32[5,2,128,128]{3,2,0,1:T(8,128)S(1)}, f32[5,2,128,128]{3,2,0,1:T(8,128)S(1)}, u32[]{:S(2)}, u32[]{:S(2)}) collective-permute-start(f32[5,2,128,128]{3,2,0,1:T(8,128)S(1)} %maximum_select_fusion.4), channel_id=1, source_target_pairs={{0,16},{1,17},{2,18},{3,19},{4,20},{5,21},{6,22},{7,23},{8,24},{9,... | collective-permute-start | bytes 1966088 | tf_op jit(solution)/shard_map/ppermute | solution.py:15
  366.7 2.9 copy-start.2
  369.6 172.4 %all-reduce.14.cloned.1.call-start = ((), (), s32[]{:S(2)}) async-start(), calls=%async_computation.1 | async-start | bytes 131072 | tf_op jit(solution)/shard_map/psum | solution.py:128
  478.9 146.9 %all-reduce.22.cloned.1.call-start = ((), (), s32[]{:S(2)}) async-start(), calls=%async_computation.5 | async-start | bytes 1310720 | tf_op jit(solution)/shard_map/psum | solution.py:20
  544.5 15.4 %copy-start = (f32[20,128,128]{2,1,0:T(8,128)}, f32[20,128,128]{2,1,0:T(8,128)S(1)}, u32[]{:S(2)}) copy-start(f32[20,128,128]{2,1,0:T(8,128)S(1)} %convolution_add_fusion) | copy-start | bytes 3932164
  560.0 259.8 %all-reduce.16.cloned.1.call-start = ((), (), s32[]{:S(2)}) async-start(), calls=%async_computation.2 | async-start | bytes 2621440 | tf_op jit(solution)/shard_map/psum | solution.py:103
  625.8 29.1 %copy-start.4 = (f32[640,128]{1,0:T(8,128)S(1)}, f32[640,128]{1,0:T(8,128)}, u32[]{:S(2)}) copy-start(f32[640,128]{1,0:T(8,128)} %get-tuple-element.4) | copy-start | bytes 983044
  625.8 6.7 collective-permute-start.10
  632.6 15.8 %collective-permute-start.11 = (f32[5,128,128]{2,1,0:T(8,128)S(1)}, f32[5,128,128]{2,1,0:T(8,128)S(1)}, u32[]{:S(2)}, u32[]{:S(2)}) collective-permute-start(f32[5,128,128]{2,1,0:T(8,128)S(1)} %broadcast_select_fusion), channel_id=1, source_target_pairs={{0,2},{1,3},{2,0},{3,1},{4,6},{5,7},{6,4},{7,5},{8,10},{9,11},{10,... | collective-permute-start | bytes 983048 | tf_op jit(solution)/shard_map/ppermute | solution.py:15
  648.4 18.6 %collective-permute-start.12 = (f32[5,128,128]{2,1,0:T(8,128)S(1)}, f32[5,128,128]{2,1,0:T(8,128)S(1)}, u32[]{:S(2)}, u32[]{:S(2)}) collective-permute-start(f32[5,128,128]{2,1,0:T(8,128)S(1)} %broadcast_select_fusion.3), channel_id=1, source_target_pairs={{0,4},{1,5},{2,6},{3,7},{4,0},{5,1},{6,2},{7,3},{8,12},{9,13},{10,... | collective-permute-start | bytes 983048 | tf_op jit(solution)/shard_map/ppermute | solution.py:15
  665.0 223.6 %all-reduce.18.cloned.1.call-start = ((), (), s32[]{:S(2)}) async-start(), calls=%async_computation.3 | async-start | bytes 131072 | tf_op jit(solution)/shard_map/psum | solution.py:128
  667.1 6.0 collective-permute-start.13
  673.1 21.0 %collective-permute-start.14 = (f32[5,2,128,128]{3,2,0,1:T(8,128)S(1)}, f32[5,2,128,128]{3,2,0,1:T(8,128)S(1)}, u32[]{:S(2)}, u32[]{:S(2)}) collective-permute-start(f32[5,2,128,128]{3,2,0,1:T(8,128)S(1)} %maximum_select_fusion.5), channel_id=1, source_target_pairs={{0,16},{1,17},{2,18},{3,19},{4,20},{5,21},{6,22},{7,23},{8,24},{9,... | collective-permute-start | bytes 1966088 | tf_op jit(solution)/shard_map/ppermute | solution.py:15
  819.8 2.1 copy-start.1
  824.9 88.4 %copy-start.6 = (f32[128,128]{1,0:T(8,128)S(1)}, f32[128,128]{1,0:T(8,128)}, u32[]{:S(2)}) copy-start(f32[128,128]{1,0:T(8,128)} %all-reduce.14.cloned.1.call-done) | copy-start | bytes 196612
  824.9 160.4 %all-reduce.20.cloned.1.call-start = ((), (), s32[]{:S(2)}) async-start(), calls=%async_computation.4 | async-start | bytes 1310720 | tf_op jit(solution)/shard_map/psum | solution.py:20
  913.8 2.6 copy-start.3
Sparse Core Ops, SparseCore 0:
  104.0 66.7 all-reduce.25
  210.2 154.6 all-reduce.11
  369.7 64.2 all-reduce.23
  479.0 62.9 all-reduce.13
  560.1 65.6 all-reduce.21
  665.2 154.6 all-reduce.15
  825.0 63.5 all-reduce.17
  919.8 65.4 all-reduce.19
where the time goes:
time: 1000 us; the launch traced here: 995 us
  waiting for transfers between devices  748 us (75%)
  other arithmetic  105 us (10%)
  matrix products  72.8 us (7%)
  starting transfers between devices  46.8 us (5%)
  between operations  14.9 us (1%)
    psum x2, waiting for transfers between devices, rows_whole(): return lax.psum(by_rows, 'col').reshape(shape_out)  249 us
    psum x3, waiting for transfers between devices, spread(): return lax.psum(kept, axis)  198 us
    psum x3, waiting for transfers between devices, reduce_grams(): return lax.psum(stacked, 'row')  177 us
    ppermute x15, waiting for transfers between devices, partner_2(): return lax.ppermute(value, axis, pairs)  123 us
    ppermute x15, starting transfers between devices, partner_2(): return lax.ppermute(value, axis, pairs)  45.8 us
    another operation x9, other arithmetic, solve_spd(): factor = jnp.linalg.cholesky(matrix)  37.2 us
    another operation x6, other arithmetic, solve_spd(): return jax.scipy.linalg.cho_solve((factor, True), target)  31.4 us
    dot_general x2, matrix products, local_products(): jnp.einsum('nm,nk->mk', lower_part, row_set.reshape(-1, columns_n), preci...  29.2 us
  transfers between devices with their start and end apart: 23, of which 22 were waited for; matrix products, arithmetic and copies ran while one was open for 6% of the time, Pallas kernels for 0%

commit v1 on v0

v1 whole, which is shorter than its diff:
```python
import functools

import jax
import jax.numpy as jnp
from jax import lax
from jax.experimental import pallas as pl
from jax.experimental.pallas import tpu as pltpu
from jax.sharding import PartitionSpec as P

MESH = pl.DeviceIdType.MESH
HIGHEST = lax.Precision.HIGHEST
F32 = jnp.float32
BF16 = jnp.bfloat16

ROWS = 8
XS = 4
ZS = 8
NBC = 5
BS = 128
K = 128
SET = NBC * BS
PART = SET // ROWS
GP = K // ROWS


def dot(a, b):
    return jnp.dot(a, b, precision=HIGHEST, preferred_element_type=F32)


def dot_t(a, b):
    return lax.dot_general(
        a, b, (((0,), (0,)), ((), ())), precision=HIGHEST, preferred_element_type=F32
    )


def halves(value):
    high = value.astype(BF16)
    low = (value - high.astype(F32)).astype(BF16)
    return high, low


def kernel(
    stored, rhs, out_x, out_r,
    araw, ahi, alo, cb, cw, cv, chl, rb, rw, rt, yt,
    p, rx, q, rz, yv, ry, own,
    gsrc, grs, gfull, gz, gx, mat,
    ld_sem, snd, snd0, rb_z, rb_x, x_sem, z_sem, y_sem, c_sem, rw_z, rw_x,
    grs_sem, gag_sem, gz_sem, gx_sem,
):
    r = lax.axis_index("row")
    c = lax.axis_index("col")
    x = c // ZS
    z = lax.rem(c, ZS)
    diagonal = r == z

    def send(src, dst, ssem, rsem, row, xx, zz):
        pltpu.make_async_remote_copy(
            src_ref=src, dst_ref=dst, send_sem=ssem, recv_sem=rsem,
            device_id=(row, xx * ZS + zz), device_id_type=MESH,
        ).start()

    def await_bytes(ref, sem):
        pltpu.make_async_copy(ref, ref, sem).wait()

    def await_sent(sem, rows):
        part = araw.at[pl.ds(0, rows)]
        pltpu.make_async_copy(part, part, sem).wait()

    load_b = pltpu.make_async_copy(rhs, cb, ld_sem.at[NBC])
    load_b.start()
    span = XS * SET

    def load_a(b):
        rows = pl.ds(b * span, span)
        return pltpu.make_async_copy(stored.at[rows], araw.at[rows], ld_sem.at[b])

    for b in range(NBC):
        load_a(b).start()

    barrier = pltpu.get_barrier_semaphore()

    def greet(row, xx, zz):
        pl.semaphore_signal(barrier, inc=1, device_id=(row, xx * ZS + zz), device_id_type=MESH)

    @pl.loop(1, 8)
    def _(k):
        greet(r, x, lax.rem(z + k, ZS))
        greet(lax.rem(r + k, ROWS), x, z)
        greet(z, x, lax.rem(z + k, ZS))
        greet(lax.rem(r + k, ROWS), x, r)

    @pl.loop(1, XS)
    def _(k):
        greet(r, lax.rem(x + k, XS), z)

    @pl.when(jnp.logical_not(diagonal))
    def _():
        greet(z, x, z)
        greet(r, x, r)
        pl.semaphore_wait(barrier, 33)

    @pl.when(diagonal)
    def _():
        pl.semaphore_wait(barrier, 31)

    load_b.wait()

    def to_z(dst_of, sem, rsem):

        @pl.loop(1, ZS)
        def _(k):
            t = lax.rem(z + k, ZS)
            s_ref, d_ref = dst_of(t)
            send(s_ref, d_ref, sem, rsem.at[z], r, x, t)

    def to_x(dst_of, sem, rsem):
        @pl.loop(1, XS)
        def _(k):
            t = lax.rem(x + k, XS)
            s_ref, d_ref = dst_of(t)
            send(s_ref, d_ref, sem, rsem.at[x], r, t, z)

    def to_r(dst_of, sem, rsem):
        @pl.loop(1, ROWS)
        def _(k):
            t = lax.rem(r + k, ROWS)
            s_ref, d_ref = dst_of(t)
            send(s_ref, d_ref, sem, rsem.at[r], t, x, z)

    def with_own(first, rest, src, dst, ssem0, rsem):
        @pl.when(diagonal)
        def _():
            pltpu.make_async_copy(src, dst, rsem).start()

        @pl.when(jnp.logical_not(diagonal))
        def _():
            send(src, dst, ssem0, rsem, *first)

        rest()

    def to_cross(src_of, dst, ssem, ssem0, rsem):
        def rest():
            @pl.loop(1, ZS)
            def _(k):
                t = lax.rem(z + k, ZS)
                send(src_of(t), dst, ssem, rsem.at[r], z, x, t)

        with_own((z, x, z), rest, src_of(z), dst, ssem0, rsem.at[r])

    def to_column(src, dst, ssem, ssem0, rsem):
        def rest():
            @pl.loop(1, ROWS)
            def _(k):
                t = lax.rem(r + k, ROWS)
                send(src, dst, ssem, rsem.at[z], t, x, r)

        with_own((r, x, r), rest, src, dst, ssem0, rsem.at[z])

    def part_rows(j):
        return pl.ds(pl.multiple_of(j * PART, 8), PART)

    def small_rows(j):
        return pl.ds(pl.multiple_of(j * GP, 8), GP)

    def split_columns(source):
        high, low = halves(source[...])
        chl[:, :K] = high
        chl[:, K:] = low

    def products_by_rows(m):
        for b in range(NBC):
            depth = (b + 1) * BS
            right = chl[:depth, :]
            both = jnp.dot(ahi[b, :, :depth], right, preferred_element_type=F32) + jnp.dot(
                alo[b, :, :depth], right, preferred_element_type=F32
            )
            total = both[:, :K] + both[:, K:]
            for xx in range(XS):
                p[m, xx, b * BS : (b + 1) * BS, :] = total[xx * BS : (xx + 1) * BS, :]

    def turn_rows(source):
        for b in range(NBC):

            @pl.loop(0, XS)
            def _(xx):
                high, low = halves(source[xx, b * BS : (b + 1) * BS, :].T)
                at = pl.ds(pl.multiple_of(xx * BS, BS), BS)
                rt[b, :K, at] = high
                rt[b, K:, at] = low

    def products_by_columns(m):
        for b in reversed(range(NBC)):
            depth = (b + 1) * BS
            left = rt[b]
            both = jnp.dot(left, ahi[b, :, :depth], preferred_element_type=F32) + jnp.dot(
                left, alo[b, :, :depth], preferred_element_type=F32
            )
            total = both[:K, :] + both[K:, :]
            if b == NBC - 1:
                yt[...] = total
            else:
                yt[:, :depth] += total
        for b in range(NBC):
            yv[m, b * BS : (b + 1) * BS, :] = yt[:, b * BS : (b + 1) * BS].T

    def gram_rows(left, right):
        def step(xx, total):
            return total + dot_t(left[xx], right[xx])

        return lax.fori_loop(0, XS, step, jnp.zeros((K, K), F32))

    def invert(source):
        mat[...] = source
        lanes = lax.broadcasted_iota(jnp.int32, (K, K), 1)
        subs = lax.broadcasted_iota(jnp.int32, (K, K), 0)
        lane_row = lax.broadcasted_iota(jnp.int32, (1, K), 1)

        @pl.loop(0, K)
        def _(j):
            row = mat[pl.ds(j, 1), :]
            now = mat[...]
            in_col = lanes == j
            col = jnp.sum(jnp.where(in_col, now, 0.0), axis=1, keepdims=True)
            pivot = jnp.sum(jnp.where(lane_row == j, row, 0.0), axis=1, keepdims=True)
            scaled = jnp.where(lane_row == j, 1.0, row) / pivot
            mat[...] = jnp.where(subs == j, scaled, jnp.where(in_col, 0.0, now) - col * scaled)

        return mat[...]

    def sum_start(k, value, sem):
        gsrc[k] = value
        to_r(lambda t: (gsrc.at[k, small_rows(t)], grs.at[k, r]), sem, grs_sem.at[k])

    def sum_middle(k):
        grs[k, r] = gsrc[k, small_rows(r)]

        @pl.loop(1, ROWS)
        def _(j):
            t = lax.rem(r + j, ROWS)
            await_bytes(grs.at[k, t], grs_sem.at[k, t])

        total = grs[k, 0]
        for j in range(1, ROWS):
            total = total + grs[k, j]
        return total

    def sum_spread(k, total, sem):
        gfull[k, small_rows(r)] = total
        piece = gfull.at[k, small_rows(r)]
        to_r(lambda t: (piece, piece), sem, gag_sem.at[k])

    def sum_end(k):
        @pl.loop(1, ROWS)
        def _(j):
            t = lax.rem(r + j, ROWS)
            await_bytes(gfull.at[k, small_rows(t)], gag_sem.at[k, t])

        return gfull[k]

    to_cross(
        lambda t: cb.at[part_rows(r)], rb.at[x, part_rows(r)], snd.at[0], snd0.at[0], rb_z
    )
    split_columns(cb)

    mine = x * ZS + z
    for b in range(NBC):
        load_a(b).wait()

        @pl.loop(0, XS)
        def _(xx):
            there = xx * ZS + r
            weight = jnp.where(there > mine, 1.0, jnp.where(there == mine, 0.5, 0.0)).astype(F32)
            at = pl.ds(pl.multiple_of(xx * BS, BS), BS)
            for bb in range(b + 1):
                block = araw[pl.ds((b * XS + xx) * SET + bb, BS, NBC), :]
                if bb == b:
                    block = block * weight
                high, low = halves(block)
                ahi[b, at, bb * BS : (bb + 1) * BS] = high
                alo[b, at, bb * BS : (bb + 1) * BS] = low

    def scatter_rows(m):
        to_x(lambda t: (p.at[m, t], rx.at[m, x]), snd.at[1 + m], x_sem.at[m])

    def scatter_rows_next(m):
        @pl.loop(1, XS)
        def _(k):
            t = lax.rem(x + k, XS)
            await_bytes(rx.at[m, t], x_sem.at[m, t])

        rx[m, x] = p[m, x]
        q[m] = (rx[m, 0] + rx[m, 1]) + (rx[m, 2] + rx[m, 3])
        to_z(lambda t: (q.at[m, part_rows(t)], rz.at[m, z]), snd.at[3 + m], z_sem.at[m])

    def scatter_columns(m):
        to_cross(
            lambda t: yv.at[m, part_rows(t)], ry.at[m, r], snd.at[5 + m], snd0.at[1 + m], y_sem.at[m]
        )

    def owned(m):
        rz[m, z] = q[m, part_rows(z)]

        @pl.loop(1, ZS)
        def _(k):
            t = lax.rem(z + k, ZS)
            await_bytes(rz.at[m, t], z_sem.at[m, t])

        @pl.loop(0, ROWS)
        def _(k):
            await_bytes(ry.at[m, k], y_sem.at[m, k])

        total = rz[m, 0] + ry[m, 0]
        for j in range(1, 8):
            total = total + (rz[m, j] + ry[m, j])
        own[m] = total

    def gather_columns(m, dst):
        to_column(
            own.at[m], dst.at[part_rows(z)], snd.at[7 + m], snd0.at[3 + m], c_sem.at[m]
        )

    def columns_here(m, dst):
        @pl.loop(0, ZS)
        def _(k):
            await_bytes(dst.at[part_rows(k)], c_sem.at[m, k])

    products_by_rows(0)
    scatter_rows(0)

    @pl.loop(0, ROWS)
    def _(k):
        await_bytes(rb.at[x, part_rows(k)], rb_z.at[k])

    to_x(lambda t: (rb.at[x], rb.at[x]), snd.at[9], rb_x)

    @pl.loop(1, XS)
    def _(k):
        t = lax.rem(x + k, XS)
        await_bytes(rb.at[t], rb_x.at[t])

    turn_rows(rb)
    products_by_columns(0)
    scatter_columns(0)
    sum_start(0, gram_rows(rb, rb), snd.at[10])
    scatter_rows_next(0)
    sum_spread(0, sum_middle(0), snd.at[11])
    gram0 = sum_end(0)
    gram0_inverse = invert(gram0)
    gsrc[4] = gram0_inverse
    owned(0)

    gather_columns(0, cw)
    rw[x, part_rows(z)] = own[0]
    to_z(lambda t: (own.at[0], rw.at[x, part_rows(z)]), snd.at[12], rw_z)
    columns_here(0, cw)
    split_columns(cw)
    products_by_rows(1)

    @pl.loop(1, ZS)
    def _(k):
        t = lax.rem(z + k, ZS)
        await_bytes(rw.at[x, part_rows(t)], rw_z.at[t])

    to_x(lambda t: (rw.at[x], rw.at[x]), snd.at[13], rw_x)
    scatter_rows(1)

    @pl.loop(1, XS)
    def _(k):
        t = lax.rem(x + k, XS)
        await_bytes(rw.at[t], rw_x.at[t])

    sum_start(1, gram_rows(rb, rw), snd.at[14])
    turn_rows(rw)
    products_by_columns(1)
    scatter_columns(1)
    scatter_rows_next(1)
    sum_spread(1, sum_middle(1), snd.at[15])
    curvature = sum_end(1)
    step = dot(invert(curvature), gfull[0])

    def residual_gram(xx, total):
        part = rb[xx] - dot(rw[xx], step)
        return total + dot_t(part, part)

    sum_start(2, lax.fori_loop(0, XS, residual_gram, jnp.zeros((K, K), F32)), snd.at[16])
    sum_spread(2, sum_middle(2), snd.at[17])
    gram1 = sum_end(2)
    mix = dot(gsrc[4], gram1)
    owned(1)
    gather_columns(1, cv)

    def image_of(wide, wider):
        return wide + dot(wide, mix) - dot(wider, step)

    b_own = rb[x, part_rows(z)]
    d_own = b_own - dot(own[0], step) + dot(b_own, mix)
    sum_start(3, dot_t(d_own, image_of(own[0], own[1])), snd.at[18])
    gz[z] = sum_middle(3)
    to_z(lambda t: (gz.at[z], gz.at[z]), snd.at[19], gz_sem)

    @pl.loop(1, ZS)
    def _(k):
        t = lax.rem(z + k, ZS)
        await_bytes(gz.at[t], gz_sem.at[t])

    total = gz[0]
    for j in range(1, ZS):
        total = total + gz[j]
    gx[x] = total
    to_x(lambda t: (gx.at[x], gx.at[x]), snd.at[20], gx_sem)

    @pl.loop(1, XS)
    def _(k):
        t = lax.rem(x + k, XS)
        await_bytes(gx.at[t], gx_sem.at[t])

    sum_spread(3, (gx[0] + gx[1]) + (gx[2] + gx[3]), snd.at[21])
    curvature2 = sum_end(3)
    step2 = dot(invert(curvature2), gfull[2])
    columns_here(1, cv)
    res = cb[...] - dot(cw[...], step)
    direction = res + dot(cb[...], mix)
    out_x[...] = dot(cb[...], step) + dot(direction, step2)
    out_r[...] = res - dot(image_of(cw[...], cv[...]), step2)

    small = 7 * GP
    for index, rows in (
        (0, 7 * PART), (1, 3 * SET), (2, 3 * SET), (3, 7 * PART), (4, 7 * PART),
        (5, 7 * PART), (6, 7 * PART), (7, 7 * PART), (8, 7 * PART), (9, 3 * SET),
        (10, small), (11, small), (12, 7 * PART), (13, 3 * SET), (14, small), (15, small),
        (16, small), (17, small), (18, small), (19, small), (20, 3 * GP), (21, small),
    ):
        await_sent(snd.at[index], rows)

    @pl.when(jnp.logical_not(diagonal))
    def _():
        for index in range(5):
            await_sent(snd0.at[index], PART)


def per_device(stored, rhs):
    vm = pltpu.VMEM
    dma = pltpu.SemaphoreType.DMA
    outs = pl.pallas_call(
        kernel,
        out_shape=(jax.ShapeDtypeStruct((SET, K), F32), jax.ShapeDtypeStruct((SET, K), F32)),
        in_specs=[pl.BlockSpec(memory_space=pl.ANY), pl.BlockSpec(memory_space=pl.ANY)],
        out_specs=(pl.BlockSpec(memory_space=pltpu.VMEM), pl.BlockSpec(memory_space=pltpu.VMEM)),
        scratch_shapes=[
            vm((NBC * XS * SET, BS), F32),
            vm((NBC, XS * BS, SET), BF16),
            vm((NBC, XS * BS, SET), BF16),
            vm((SET, K), F32),
            vm((SET, K), F32),
            vm((SET, K), F32),
            vm((SET, 2 * K), BF16),
            vm((XS, SET, K), F32),
            vm((XS, SET, K), F32),
            vm((NBC, 2 * K, XS * BS), BF16),
            vm((K, SET), F32),
            vm((2, XS, SET, K), F32),
            vm((2, XS, SET, K), F32),
            vm((2, SET, K), F32),
            vm((2, ZS, PART, K), F32),
            vm((2, SET, K), F32),
            vm((2, ROWS, PART, K), F32),
            vm((2, PART, K), F32),
            vm((5, K, K), F32),
            vm((4, ROWS, GP, K), F32),
            vm((4, K, K), F32),
            vm((ZS, GP, K), F32),
            vm((XS, GP, K), F32),
            vm((K, K), F32),
            dma((NBC + 1,)),
            dma((22,)),
            dma((5,)),
            dma((ROWS,)),
            dma((XS,)),
            dma((2, XS)),
            dma((2, ZS)),
            dma((2, ROWS)),
            dma((2, ZS)),
            dma((ZS,)),
            dma((XS,)),
            dma((4, ROWS)),
            dma((4, ROWS)),
            dma((ZS,)),
            dma((XS,)),
        ],
        compiler_params=pltpu.CompilerParams(
            collective_id=0, has_side_effects=True, vmem_limit_bytes=56 * 2**20
        ),
        name="block_cg",
    )(stored.reshape(-1, BS), rhs.reshape(-1, K))
    return tuple(o.reshape(rhs.shape) for o in outs)


def solution(mesh):
    return jax.shard_map(
        per_device,
        mesh=mesh,
        in_specs=(P(None, "row", None, None, "col", None), P(None, "col", None, None)),
        out_specs=(P(None, "col", None, None), P(None, "col", None, None)),
        check_vma=False,
    )
```

time: 1000 us -> 218 us (0.22)
  waiting for transfers between devices: 748 us -> 0 us
  Pallas kernels: 0 us -> 214 us
  other arithmetic: 105 us -> 0 us
  matrix products: 72.8 us -> 0 us
  starting transfers between devices: 46.8 us -> 0 us
  between operations: 14.9 us -> 0.64 us
    psum x8 -> x0, waiting for transfers between devices: 624 us -> none  [the longest x2 249 us: rows_whole(): return lax.psum(by_rows, 'col').reshape(shape_out)]
    pallas_call x0 -> x1, Pallas kernels: none -> 214 us  [per_device(): pl.pallas_call(kernel, out_shape=(jax.ShapeDtypeStruct((SET, K), F32), ja...]
    ppermute x15 -> x0, waiting for transfers between devices: 123 us -> none  [partner_2(): return lax.ppermute(value, axis, pairs)]
    dot_general x13 -> x0, matrix products: 69.7 us -> none  [the longest x2 29.2 us: local_products(): jnp.einsum('nm,nk->mk', lower_part, row_set.reshape(-1, columns_n), preci...]
    another operation x15 -> x0, other arithmetic: 68.6 us -> none  [the longest x9 37.2 us: solve_spd(): factor = jnp.linalg.cholesky(matrix)]
    ppermute x15 -> x0, starting transfers between devices: 45.8 us -> none  [partner_2(): return lax.ppermute(value, axis, pairs)]
    mul x1 -> x0, other arithmetic: 23.9 us -> none  [per_device(): stored.reshape(row_blocks, block_size, col_blocks, block_size)]
  transfers between devices with their start and end apart: 23 -> 0, of which waited for: 22 -> 0; matrix products, arithmetic and copies ran while one was open for 6% -> 0% of each run, Pallas kernels for 0% -> 0%
where the time goes in v1:
time: 218 us
  Pallas kernels  214 us (98%)
  local copies, waits for them, and re-layouts  3.44 us (2%)
    pallas_call x1, Pallas kernels, per_device(): pl.pallas_call(kernel, out_shape=(jax.ShapeDtypeStruct((SET, K), F32), ja...  214 us

profile of v1, /device:TPU:1, one launch (start us, length us, event | category | flops | bytes accessed | tf_op | source)
XLA Modules:
  0.0 218.0 jit_solution(12657263931887229314)
XLA Ops:
  0.6 213.9 %block_cg.1 = (f32[640,128]{1,0:T(8,128)}, f32[640,128]{1,0:T(8,128)}) custom-call(f32[12800,128]{1,0:T(8,128)} %bitcast.8, f32[640,128]{1,0:T(8,128)} %bitcast.11), custom_call_target="tpu_custom_call" | custom-call | tf_op jit(solution)/shard_map/block_cg/pallas_call | solution.py:444
  214.5 1.7 copy.8
  216.2 1.7 copy.9

commit v2 on v1

--- a/solution.py
+++ b/solution.py
@@ -21,6 +21,8 @@
 SET = NBC * BS
 PART = SET // ROWS
 GP = K // ROWS
+FOUR = 4
+WIDE = 20
 
 
 def dot(a, b):
@@ -42,9 +44,9 @@
 def kernel(
     stored, rhs, out_x, out_r,
     araw, ahi, alo, cb, cw, cv, chl, rb, rw, rt, yt,
-    p, rx, q, rz, yv, ry, own,
-    gsrc, grs, gfull, gz, gx, mat,
-    ld_sem, snd, snd0, rb_z, rb_x, x_sem, z_sem, y_sem, c_sem, rw_z, rw_x,
+    p, rx, q, rz, yv, ry, own, swapped,
+    gsrc, grs, gfull, gz, gx, mat, cres, cdir, cimg,
+    ld_sem, snd, snd0, rb_z, rb_x, x_sem, z_sem, y_sem, c_sem, w_sem, rw_z, rw_x,
     grs_sem, gag_sem, gz_sem, gx_sem,
 ):
     r = lax.axis_index("row")
@@ -86,7 +88,6 @@
     def _(k):
         greet(r, x, lax.rem(z + k, ZS))
         greet(lax.rem(r + k, ROWS), x, z)
-        greet(z, x, lax.rem(z + k, ZS))
         greet(lax.rem(r + k, ROWS), x, r)
 
     @pl.loop(1, XS)
@@ -95,13 +96,12 @@
 
     @pl.when(jnp.logical_not(diagonal))
     def _():
-        greet(z, x, z)
         greet(r, x, r)
-        pl.semaphore_wait(barrier, 33)
+        pl.semaphore_wait(barrier, 25)
 
     @pl.when(diagonal)
     def _():
-        pl.semaphore_wait(barrier, 31)
+        pl.semaphore_wait(barrier, 24)
 
     load_b.wait()
 
@@ -146,15 +146,6 @@
                 send(src_of(t), dst, ssem, rsem.at[r], z, x, t)
 
         with_own((z, x, z), rest, src_of(z), dst, ssem0, rsem.at[r])
-
-    def to_column(src, dst, ssem, ssem0, rsem):
-        def rest():
-            @pl.loop(1, ROWS)
-            def _(k):
-                t = lax.rem(r + k, ROWS)
-                send(src, dst, ssem, rsem.at[z], t, x, r)
-
-        with_own((r, x, r), rest, src, dst, ssem0, rsem.at[z])
 
     def part_rows(j):
         return pl.ds(pl.multiple_of(j * PART, 8), PART)
@@ -209,23 +200,51 @@
 
         return lax.fori_loop(0, XS, step, jnp.zeros((K, K), F32))
 
-    def invert(source):
-        mat[...] = source
-        lanes = lax.broadcasted_iota(jnp.int32, (K, K), 1)
-        subs = lax.broadcasted_iota(jnp.int32, (K, K), 0)
-        lane_row = lax.broadcasted_iota(jnp.int32, (1, K), 1)
-
-        @pl.loop(0, K)
-        def _(j):
-            row = mat[pl.ds(j, 1), :]
-            now = mat[...]
-            in_col = lanes == j
-            col = jnp.sum(jnp.where(in_col, now, 0.0), axis=1, keepdims=True)
-            pivot = jnp.sum(jnp.where(lane_row == j, row, 0.0), axis=1, keepdims=True)
-            scaled = jnp.where(lane_row == j, 1.0, row) / pivot
-            mat[...] = jnp.where(subs == j, scaled, jnp.where(in_col, 0.0, now) - col * scaled)
-
-        return mat[...]
+    lanes = lax.broadcasted_iota(jnp.int32, (K, K), 1)
+    subs = lax.broadcasted_iota(jnp.int32, (K, K), 0)
+    lane_row = lax.broadcasted_iota(jnp.int32, (1, K), 1)
+
+    def eliminate(now, rows, first):
+        hits = [lane_row == first + a for a in range(FOUR)]
+        any_hit = hits[0] | hits[1] | hits[2] | hits[3]
+        cols = [
+            jnp.sum(jnp.where(lanes == first + a, now, 0.0), axis=1, keepdims=True)
+            for a in range(FOUR)
+        ]
+        block = [
+            [jnp.sum(jnp.where(h, row, 0.0), axis=1, keepdims=True) for h in hits] for row in rows
+        ]
+        rows = [
+            jnp.where(any_hit, jnp.where(h, 1.0, 0.0), row) for h, row in zip(hits, rows)
+        ]
+        scale = []
+        for a in range(FOUR):
+            scale.append(1.0 / block[a][a])
+            for b in range(a + 1, FOUR):
+                factor = block[b][a] * scale[a]
+                for c in range(a + 1, FOUR):
+                    block[b][c] = block[b][c] - factor * block[a][c]
+                rows[b] = rows[b] - factor * rows[a]
+        for a in reversed(range(FOUR)):
+            for b in range(a + 1, FOUR):
+                rows[a] = rows[a] - block[a][b] * rows[b]
+            rows[a] = rows[a] * scale[a]
+        now = jnp.where((lanes >= first) & (lanes < first + FOUR), 0.0, now)
+        for a in range(FOUR):
+            now = now - cols[a] * rows[a]
+        for a in range(FOUR):
+            now = jnp.where(subs == first + a, rows[a], now)
+        return now
+
+    def pivots(slots, first, last):
+        @pl.loop(first // FOUR, last // FOUR)
+        def _(i):
+            done = [
+                eliminate(mat[s], [mat[s, pl.ds(FOUR * i + a, 1), :] for a in range(FOUR)], FOUR * i)
+                for s in slots
+            ]
+            for s, value in zip(slots, done):
+                mat[s] = value
 
     def sum_start(k, value, sem):
         gsrc[k] = value
@@ -256,6 +275,30 @@
             await_bytes(gfull.at[k, small_rows(t)], gag_sem.at[k, t])
 
         return gfull[k]
+
+    def wide_z(k):
+        gz[k, z] = sum_middle(k)
+        to_z(lambda t: (gz.at[k, z], gz.at[k, z]), snd.at[WIDE + 2 * k], gz_sem.at[k])
+
+    def wide_x(k):
+        @pl.loop(1, ZS)
+        def _(j):
+            t = lax.rem(z + j, ZS)
+            await_bytes(gz.at[k, t], gz_sem.at[k, t])
+
+        total = gz[k, 0]
+        for j in range(1, ZS):
+            total = total + gz[k, j]
+        gx[k, x] = total
+        to_x(lambda t: (gx.at[k, x], gx.at[k, x]), snd.at[WIDE + 1 + 2 * k], gx_sem.at[k])
+
+    def wide_r(k, sem):
+        @pl.loop(1, XS)
+        def _(j):
+            t = lax.rem(x + j, XS)
+            await_bytes(gx.at[k, t], gx_sem.at[k, t])
+
+        sum_spread(k, (gx[k, 0] + gx[k, 1]) + (gx[k, 2] + gx[k, 3]), sem)
 
     to_cross(
         lambda t: cb.at[part_rows(r)], rb.at[x, part_rows(r)], snd.at[0], snd0.at[0], rb_z
@@ -280,17 +323,31 @@
                 alo[b, at, bb * BS : (bb + 1) * BS] = low
 
     def scatter_rows(m):
-        to_x(lambda t: (p.at[m, t], rx.at[m, x]), snd.at[1 + m], x_sem.at[m])
-
-    def scatter_rows_next(m):
-        @pl.loop(1, XS)
-        def _(k):
-            t = lax.rem(x + k, XS)
-            await_bytes(rx.at[m, t], x_sem.at[m, t])
-
-        rx[m, x] = p[m, x]
-        q[m] = (rx[m, 0] + rx[m, 1]) + (rx[m, 2] + rx[m, 3])
-        to_z(lambda t: (q.at[m, part_rows(t)], rz.at[m, z]), snd.at[3 + m], z_sem.at[m])
+        @pl.loop(1, ZS + 1)
+        def _(k):
+            at = part_rows(lax.rem(z + k, ZS))
+            sem = x_sem.at[m, x, lax.rem(z + k, ZS)]
+            for far in (1, 3, 2):
+                t = lax.rem(x + far, XS)
+                send(p.at[m, t, at], rx.at[m, x, at], snd.at[1 + m], sem, r, t, z)
+
+    def sum_x(m, slot):
+        at = part_rows(slot)
+        total = p[m, x, at]
+        for far in (1, 3, 2):
+            t = lax.rem(x + far, XS)
+            await_bytes(rx.at[m, t, at], x_sem.at[m, t, slot])
+            total = total + rx[m, t, at]
+        return total
+
+    def scatter_rows_next(m, first, last):
+        @pl.loop(first, last)
+        def _(k):
+            slot = lax.rem(z + k, ZS)
+            q[m, part_rows(slot)] = sum_x(m, slot)
+            send(
+                q.at[m, part_rows(slot)], rz.at[m, z], snd.at[3 + m], z_sem.at[m, z], r, x, slot
+            )
 
     def scatter_columns(m):
         to_cross(
@@ -298,7 +355,7 @@
         )
 
     def owned(m):
-        rz[m, z] = q[m, part_rows(z)]
+        rz[m, z] = sum_x(m, z)
 
         @pl.loop(1, ZS)
         def _(k):
@@ -314,121 +371,136 @@
             total = total + (rz[m, j] + ry[m, j])
         own[m] = total
 
-    def gather_columns(m, dst):
-        to_column(
-            own.at[m], dst.at[part_rows(z)], snd.at[7 + m], snd0.at[3 + m], c_sem.at[m]
-        )
+    def swap_start(m):
+        @pl.when(diagonal)
+        def _():
+            swapped[m] = own[m]
+
+        @pl.when(jnp.logical_not(diagonal))
+        def _():
+            send(own.at[m], swapped.at[m], snd0.at[3 + m], w_sem.at[m], z, x, r)
+
+    def swap_spread(m, dst):
+        @pl.when(jnp.logical_not(diagonal))
+        def _():
+            await_bytes(swapped.at[m], w_sem.at[m])
+
+        dst[part_rows(r)] = swapped[m]
+        piece = dst.at[part_rows(r)]
+        to_r(lambda t: (piece, piece), snd.at[7 + m], c_sem.at[m])
 
     def columns_here(m, dst):
-        @pl.loop(0, ZS)
-        def _(k):
-            await_bytes(dst.at[part_rows(k)], c_sem.at[m, k])
+        @pl.loop(1, ROWS)
+        def _(k):
+            t = lax.rem(r + k, ROWS)
+            await_bytes(dst.at[part_rows(t)], c_sem.at[m, t])
+
+    def forward(rows, slot, ssem, rsem):
+        piece = rows.at[x, part_rows(slot)]
+        for far in (1, 3, 2):
+            send(piece, piece, ssem, rsem.at[x], r, lax.rem(x + far, XS), z)
+
+    def rows_here(rows, rsem):
+        @pl.loop(1, XS)
+        def _(k):
+            t = lax.rem(x + k, XS)
+            await_bytes(rows.at[t], rsem.at[t])
 
     products_by_rows(0)
-    scatter_rows(0)
 
     @pl.loop(0, ROWS)
     def _(k):
-        await_bytes(rb.at[x, part_rows(k)], rb_z.at[k])
-
-    to_x(lambda t: (rb.at[x], rb.at[x]), snd.at[9], rb_x)
-
-    @pl.loop(1, XS)
-    def _(k):
-        t = lax.rem(x + k, XS)
-        await_bytes(rb.at[t], rb_x.at[t])
-
+        slot = lax.rem(r + k, ROWS)
+        await_bytes(rb.at[x, part_rows(slot)], rb_z.at[slot])
+        forward(rb, slot, snd.at[9], rb_x)
+
+    scatter_rows(0)
+    rows_here(rb, rb_x)
     turn_rows(rb)
     products_by_columns(0)
     scatter_columns(0)
+    sum_start(1, gram_rows(rb, p.at[0]), snd.at[14])
     sum_start(0, gram_rows(rb, rb), snd.at[10])
-    scatter_rows_next(0)
+    scatter_rows_next(0, 1, 3)
+    wide_z(1)
     sum_spread(0, sum_middle(0), snd.at[11])
-    gram0 = sum_end(0)
-    gram0_inverse = invert(gram0)
-    gsrc[4] = gram0_inverse
+    scatter_rows_next(0, 3, 5)
+    wide_x(1)
+    scatter_rows_next(0, 5, 7)
+    wide_r(1, snd.at[15])
+    scatter_rows_next(0, 7, 8)
     owned(0)
 
-    gather_columns(0, cw)
+    swap_start(0)
     rw[x, part_rows(z)] = own[0]
     to_z(lambda t: (own.at[0], rw.at[x, part_rows(z)]), snd.at[12], rw_z)
+    forward(rw, z, snd.at[13], rw_x)
+    mat[0] = sum_end(0)
+    half = sum_end(1)
+    mat[1] = half + half.T
+
+    def onward(k):
+        slot = lax.rem(z + k, ZS)
+        await_bytes(rw.at[x, part_rows(slot)], rw_z.at[slot])
+        forward(rw, slot, snd.at[13], rw_x)
+
+    chunk = K // 8
+    for k, far in enumerate((1, 7, 2, 6, 3, 5, 4)):
+        onward(far)
+        if k == 3:
+            swap_spread(0, cw)
+        pivots((0, 1), k * chunk, (k + 1) * chunk)
     columns_here(0, cw)
     split_columns(cw)
     products_by_rows(1)
-
-    @pl.loop(1, ZS)
-    def _(k):
-        t = lax.rem(z + k, ZS)
-        await_bytes(rw.at[x, part_rows(t)], rw_z.at[t])
-
-    to_x(lambda t: (rw.at[x], rw.at[x]), snd.at[13], rw_x)
     scatter_rows(1)
-
-    @pl.loop(1, XS)
-    def _(k):
-        t = lax.rem(x + k, XS)
-        await_bytes(rw.at[t], rw_x.at[t])
-
-    sum_start(1, gram_rows(rb, rw), snd.at[14])
+    pivots((0, 1), K - chunk, K)
+    step = dot(mat[1], gfull[0])
+    b_own = rb[x, part_rows(z)]
+    r_own = b_own - dot(own[0], step)
+    sum_start(2, dot_t(r_own, r_own), snd.at[16])
+    rows_here(rw, rw_x)
     turn_rows(rw)
+    wide_z(2)
     products_by_columns(1)
     scatter_columns(1)
-    scatter_rows_next(1)
-    sum_spread(1, sum_middle(1), snd.at[15])
-    curvature = sum_end(1)
-    step = dot(invert(curvature), gfull[0])
-
-    def residual_gram(xx, total):
-        part = rb[xx] - dot(rw[xx], step)
-        return total + dot_t(part, part)
-
-    sum_start(2, lax.fori_loop(0, XS, residual_gram, jnp.zeros((K, K), F32)), snd.at[16])
-    sum_spread(2, sum_middle(2), snd.at[17])
-    gram1 = sum_end(2)
-    mix = dot(gsrc[4], gram1)
+    scatter_rows_next(1, 1, 2)
+    wide_x(2)
+    scatter_rows_next(1, 2, 4)
+    wide_r(2, snd.at[17])
+    scatter_rows_next(1, 4, 8)
+    mix = dot(mat[0], sum_end(2))
     owned(1)
-    gather_columns(1, cv)
+    swap_start(1)
 
     def image_of(wide, wider):
         return wide + dot(wide, mix) - dot(wider, step)
 
-    b_own = rb[x, part_rows(z)]
-    d_own = b_own - dot(own[0], step) + dot(b_own, mix)
+    d_own = r_own + dot(b_own, mix)
     sum_start(3, dot_t(d_own, image_of(own[0], own[1])), snd.at[18])
-    gz[z] = sum_middle(3)
-    to_z(lambda t: (gz.at[z], gz.at[z]), snd.at[19], gz_sem)
-
-    @pl.loop(1, ZS)
-    def _(k):
-        t = lax.rem(z + k, ZS)
-        await_bytes(gz.at[t], gz_sem.at[t])
-
-    total = gz[0]
-    for j in range(1, ZS):
-        total = total + gz[j]
-    gx[x] = total
-    to_x(lambda t: (gx.at[x], gx.at[x]), snd.at[20], gx_sem)
-
-    @pl.loop(1, XS)
-    def _(k):
-        t = lax.rem(x + k, XS)
-        await_bytes(gx.at[t], gx_sem.at[t])
-
-    sum_spread(3, (gx[0] + gx[1]) + (gx[2] + gx[3]), snd.at[21])
-    curvature2 = sum_end(3)
-    step2 = dot(invert(curvature2), gfull[2])
+    res = cb[...] - dot(cw[...], step)
+    cres[...] = res
+    cdir[...] = res + dot(cb[...], mix)
+    wide_z(3)
+    swap_spread(1, cv)
+    wide_x(3)
+    out_x[...] = dot(cb[...], step)
+    wide_r(3, snd.at[19])
     columns_here(1, cv)
-    res = cb[...] - dot(cw[...], step)
-    direction = res + dot(cb[...], mix)
-    out_x[...] = dot(cb[...], step) + dot(direction, step2)
-    out_r[...] = res - dot(image_of(cw[...], cv[...]), step2)
+    cimg[...] = image_of(cw[...], cv[...])
+    mat[0] = sum_end(3)
+    pivots((0,), 0, K)
+    step2 = dot(mat[0], gfull[2])
+    out_x[...] += dot(cdir[...], step2)
+    out_r[...] = cres[...] - dot(cimg[...], step2)
 
     small = 7 * GP
-    for index, rows in (
+    wide = tuple((WIDE + 2 * k + j, rows) for k in (1, 2, 3) for j, rows in ((0, small), (1, 3 * GP)))
+    for index, rows in wide + (
         (0, 7 * PART), (1, 3 * SET), (2, 3 * SET), (3, 7 * PART), (4, 7 * PART),
         (5, 7 * PART), (6, 7 * PART), (7, 7 * PART), (8, 7 * PART), (9, 3 * SET),
         (10, small), (11, small), (12, 7 * PART), (13, 3 * SET), (14, small), (15, small),
-        (16, small), (17, small), (18, small), (19, small), (20, 3 * GP), (21, small),
+        (16, small), (17, small), (18, small), (19, small),
     ):
         await_sent(snd.at[index], rows)
 
@@ -465,27 +537,32 @@
             vm((2, SET, K), F32),
             vm((2, ROWS, PART, K), F32),
             vm((2, PART, K), F32),
-            vm((5, K, K), F32),
+            vm((2, PART, K), F32),
+            vm((4, K, K), F32),
             vm((4, ROWS, GP, K), F32),
             vm((4, K, K), F32),
-            vm((ZS, GP, K), F32),
-            vm((XS, GP, K), F32),
-            vm((K, K), F32),
+            vm((4, ZS, GP, K), F32),
+            vm((4, XS, GP, K), F32),
+            vm((2, K, K), F32),
+            vm((SET, K), F32),
+            vm((SET, K), F32),
+            vm((SET, K), F32),
             dma((NBC + 1,)),
-            dma((22,)),
+            dma((28,)),
             dma((5,)),
             dma((ROWS,)),
             dma((XS,)),
-            dma((2, XS)),
+            dma((2, XS, ZS)),
             dma((2, ZS)),
             dma((2, ROWS)),
-            dma((2, ZS)),
+            dma((2, ROWS)),
+            dma((2,)),
             dma((ZS,)),
             dma((XS,)),
             dma((4, ROWS)),
             dma((4, ROWS)),
-            dma((ZS,)),
-            dma((XS,)),
+            dma((4, ZS)),
+            dma((4, XS)),
         ],
         compiler_params=pltpu.CompilerParams(
             collective_id=0, has_side_effects=True, vmem_limit_bytes=56 * 2**20

time: 218 us -> 139 us (0.64)
  Pallas kernels: 214 us -> 134 us
    pallas_call x1, Pallas kernels: 214 us -> 134 us  [per_device(): pl.pallas_call(kernel, out_shape=(jax.ShapeDtypeStruct((SET, K), F32), ja...]
where the time goes in v2:
time: 139 us
  Pallas kernels  134 us (96%)
  local copies, waits for them, and re-layouts  3.44 us (2%)
    pallas_call x1, Pallas kernels, per_device(): pl.pallas_call(kernel, out_shape=(jax.ShapeDtypeStruct((SET, K), F32), ja...  134 us
    unnamed x2, local copies, waits for them, and re-layouts  3.44 us

profile of v2, /device:TPU:1, one launch (start us, length us, event | category | flops | bytes accessed | tf_op | source)
XLA Modules:
  0.0 138.5 jit_solution(3780605677137837574)
XLA Ops:
  0.6 134.5 %block_cg.1 = (f32[640,128]{1,0:T(8,128)}, f32[640,128]{1,0:T(8,128)}) custom-call(f32[12800,128]{1,0:T(8,128)} %bitcast.8, f32[640,128]{1,0:T(8,128)} %bitcast.11), custom_call_target="tpu_custom_call" | custom-call | tf_op jit(solution)/shard_map/block_cg/pallas_call | solution.py:516
  135.1 1.7 %copy.8 = f32[5,1,128,128]{3,2,1,0:T(8,128)} copy(f32[5,1,128,128]{3,2,1,0:T(8,128)} %bitcast.10) | data formatting | bytes 655360
  136.8 1.7 %copy.9 = f32[5,1,128,128]{3,2,1,0:T(8,128)} copy(f32[5,1,128,128]{3,2,1,0:T(8,128)} %bitcast.9) | data formatting | bytes 655360

commit v3 on v2

--- a/solution.py
+++ b/solution.py
@@ -322,8 +322,8 @@
                 ahi[b, at, bb * BS : (bb + 1) * BS] = high
                 alo[b, at, bb * BS : (bb + 1) * BS] = low
 
-    def scatter_rows(m):
-        @pl.loop(1, ZS + 1)
+    def scatter_rows(m, first, last):
+        @pl.loop(first, last)
         def _(k):
             at = part_rows(lax.rem(z + k, ZS))
             sem = x_sem.at[m, x, lax.rem(z + k, ZS)]
@@ -407,6 +407,7 @@
             await_bytes(rows.at[t], rsem.at[t])
 
     products_by_rows(0)
+    scatter_rows(0, 1, 3)
 
     @pl.loop(0, ROWS)
     def _(k):
@@ -414,64 +415,66 @@
         await_bytes(rb.at[x, part_rows(slot)], rb_z.at[slot])
         forward(rb, slot, snd.at[9], rb_x)
 
-    scatter_rows(0)
     rows_here(rb, rb_x)
+    scatter_rows(0, 3, ZS + 1)
     turn_rows(rb)
     products_by_columns(0)
     scatter_columns(0)
     sum_start(1, gram_rows(rb, p.at[0]), snd.at[14])
     sum_start(0, gram_rows(rb, rb), snd.at[10])
-    scatter_rows_next(0, 1, 3)
+    scatter_rows_next(0, 1, 4)
     wide_z(1)
     sum_spread(0, sum_middle(0), snd.at[11])
-    scatter_rows_next(0, 3, 5)
+    scatter_rows_next(0, 4, 8)
+    mat[0] = sum_end(0)
     wide_x(1)
-    scatter_rows_next(0, 5, 7)
-    wide_r(1, snd.at[15])
-    scatter_rows_next(0, 7, 8)
     owned(0)
 
     swap_start(0)
     rw[x, part_rows(z)] = own[0]
     to_z(lambda t: (own.at[0], rw.at[x, part_rows(z)]), snd.at[12], rw_z)
     forward(rw, z, snd.at[13], rw_x)
-    mat[0] = sum_end(0)
-    half = sum_end(1)
-    mat[1] = half + half.T
+    wide_r(1, snd.at[15])
 
     def onward(k):
         slot = lax.rem(z + k, ZS)
         await_bytes(rw.at[x, part_rows(slot)], rw_z.at[slot])
         forward(rw, slot, snd.at[13], rw_x)
 
-    chunk = K // 8
+    chunk = K // 4
     for k, far in enumerate((1, 7, 2, 6, 3, 5, 4)):
         onward(far)
         if k == 3:
             swap_spread(0, cw)
-        pivots((0, 1), k * chunk, (k + 1) * chunk)
+            half = sum_end(1)
+            mat[1] = half + half.T
+        part = k % 4 * chunk
+        pivots((k // 4,), part, part + chunk)
     columns_here(0, cw)
     split_columns(cw)
     products_by_rows(1)
-    scatter_rows(1)
-    pivots((0, 1), K - chunk, K)
+    scatter_rows(1, 1, ZS + 1)
+    pivots((1,), K - chunk, K)
     step = dot(mat[1], gfull[0])
+    rows_here(rw, rw_x)
+    turn_rows(rw)
+    products_by_columns(1)
+    scatter_columns(1)
+    scatter_rows_next(1, 1, 3)
+
+    def residual_gram(xx, total):
+        part = rb[xx] - dot(rw[xx], step)
+        return total + dot_t(part, part)
+
+    sum_start(2, lax.fori_loop(0, XS, residual_gram, jnp.zeros((K, K), F32)), snd.at[16])
+    scatter_rows_next(1, 3, 6)
+    sum_spread(2, sum_middle(2), snd.at[17])
+    scatter_rows_next(1, 6, 8)
+    owned(1)
+    swap_start(1)
+    mix = dot(mat[0], sum_end(2))
     b_own = rb[x, part_rows(z)]
     r_own = b_own - dot(own[0], step)
-    sum_start(2, dot_t(r_own, r_own), snd.at[16])
-    rows_here(rw, rw_x)
-    turn_rows(rw)
-    wide_z(2)
-    products_by_columns(1)
-    scatter_columns(1)
-    scatter_rows_next(1, 1, 2)
-    wide_x(2)
-    scatter_rows_next(1, 2, 4)
-    wide_r(2, snd.at[17])
-    scatter_rows_next(1, 4, 8)
-    mix = dot(mat[0], sum_end(2))
-    owned(1)
-    swap_start(1)
 
     def image_of(wide, wider):
         return wide + dot(wide, mix) - dot(wider, step)
@@ -495,7 +498,7 @@
     out_r[...] = cres[...] - dot(cimg[...], step2)
 
     small = 7 * GP
-    wide = tuple((WIDE + 2 * k + j, rows) for k in (1, 2, 3) for j, rows in ((0, small), (1, 3 * GP)))
+    wide = tuple((WIDE + 2 * k + j, rows) for k in (1, 3) for j, rows in ((0, small), (1, 3 * GP)))
     for index, rows in wide + (
         (0, 7 * PART), (1, 3 * SET), (2, 3 * SET), (3, 7 * PART), (4, 7 * PART),
         (5, 7 * PART), (6, 7 * PART), (7, 7 * PART), (8, 7 * PART), (9, 3 * SET),

time: 139 us -> 133 us (0.957)
  Pallas kernels: 134 us -> 129 us
    pallas_call x1, Pallas kernels: 134 us -> 129 us  [per_device(): pl.pallas_call(kernel, out_shape=(jax.ShapeDtypeStruct((SET, K), F32), ja...]
where the time goes in v3:
time: 133 us
  Pallas kernels  129 us (97%)
  local copies, waits for them, and re-layouts  3.44 us (3%)
    pallas_call x1, Pallas kernels, per_device(): pl.pallas_call(kernel, out_shape=(jax.ShapeDtypeStruct((SET, K), F32), ja...  129 us
    unnamed x2, local copies, waits for them, and re-layouts  3.44 us

profile of v3, /device:TPU:1, one launch (start us, length us, event | category | flops | bytes accessed | tf_op | source)
XLA Modules:
  0.0 133.1 jit_solution(11047239629957210166)
XLA Ops:
  0.6 129.0 %block_cg.1 = (f32[640,128]{1,0:T(8,128)}, f32[640,128]{1,0:T(8,128)}) custom-call(f32[12800,128]{1,0:T(8,128)} %bitcast.8, f32[640,128]{1,0:T(8,128)} %bitcast.11), custom_call_target="tpu_custom_call" | custom-call | tf_op jit(solution)/shard_map/block_cg/pallas_call | solution.py:519
  129.7 1.7 %copy.8 = f32[5,1,128,128]{3,2,1,0:T(8,128)} copy(f32[5,1,128,128]{3,2,1,0:T(8,128)} %bitcast.10) | data formatting | bytes 655360
  131.4 1.7 %copy.9 = f32[5,1,128,128]{3,2,1,0:T(8,128)} copy(f32[5,1,128,128]{3,2,1,0:T(8,128)} %bitcast.9) | data formatting | bytes 655360

commit v4 on v3

--- a/solution.py
+++ b/solution.py
@@ -44,9 +44,9 @@
 def kernel(
     stored, rhs, out_x, out_r,
     araw, ahi, alo, cb, cw, cv, chl, rb, rw, rt, yt,
-    p, rx, q, rz, yv, ry, own, swapped,
+    p, rx, q, rz, yv, ry, ysum, ycross, own, swapped,
     gsrc, grs, gfull, gz, gx, mat, cres, cdir, cimg,
-    ld_sem, snd, snd0, rb_z, rb_x, x_sem, z_sem, y_sem, c_sem, w_sem, rw_z, rw_x,
+    ld_sem, snd, snd0, rb_z, rb_x, x_sem, z_sem, y_sem, c_sem, w_sem, yx_sem, rw_z, rw_x,
     grs_sem, gag_sem, gz_sem, gx_sem,
 ):
     r = lax.axis_index("row")
@@ -97,11 +97,6 @@
     @pl.when(jnp.logical_not(diagonal))
     def _():
         greet(r, x, r)
-        pl.semaphore_wait(barrier, 25)
-
-    @pl.when(diagonal)
-    def _():
-        pl.semaphore_wait(barrier, 24)
 
     load_b.wait()
 
@@ -300,9 +295,6 @@
 
         sum_spread(k, (gx[k, 0] + gx[k, 1]) + (gx[k, 2] + gx[k, 3]), sem)
 
-    to_cross(
-        lambda t: cb.at[part_rows(r)], rb.at[x, part_rows(r)], snd.at[0], snd0.at[0], rb_z
-    )
     split_columns(cb)
 
     mine = x * ZS + z
@@ -350,25 +342,46 @@
             )
 
     def scatter_columns(m):
-        to_cross(
-            lambda t: yv.at[m, part_rows(t)], ry.at[m, r], snd.at[5 + m], snd0.at[1 + m], y_sem.at[m]
+        to_r(
+            lambda t: (yv.at[m, part_rows(t)], ry.at[m, r]), snd.at[5 + m], y_sem.at[m]
         )
+
+    def columns_sum(m):
+        ry[m, r] = yv[m, part_rows(r)]
+
+        @pl.loop(1, ROWS)
+        def _(k):
+            t = lax.rem(r + k, ROWS)
+            await_bytes(ry.at[m, t], y_sem.at[m, t])
+
+        total = ry[m, 0]
+        for j in range(1, ROWS):
+            total = total + ry[m, j]
+        ysum[m] = total
+
+        @pl.when(diagonal)
+        def _():
+            ycross[m] = ysum[m]
+
+        @pl.when(jnp.logical_not(diagonal))
+        def _():
+            send(ysum.at[m], ycross.at[m], snd0.at[1 + m], yx_sem.at[m], z, x, r)
 
     def owned(m):
         rz[m, z] = sum_x(m, z)
 
+        @pl.when(jnp.logical_not(diagonal))
+        def _():
+            await_bytes(ycross.at[m], yx_sem.at[m])
+
         @pl.loop(1, ZS)
         def _(k):
             t = lax.rem(z + k, ZS)
             await_bytes(rz.at[m, t], z_sem.at[m, t])
 
-        @pl.loop(0, ROWS)
-        def _(k):
-            await_bytes(ry.at[m, k], y_sem.at[m, k])
-
-        total = rz[m, 0] + ry[m, 0]
+        total = rz[m, 0] + ycross[m]
         for j in range(1, 8):
-            total = total + (rz[m, j] + ry[m, j])
+            total = total + rz[m, j]
         own[m] = total
 
     def swap_start(m):
@@ -407,6 +420,18 @@
             await_bytes(rows.at[t], rsem.at[t])
 
     products_by_rows(0)
+
+    @pl.when(jnp.logical_not(diagonal))
+    def _():
+        pl.semaphore_wait(barrier, 25)
+
+    @pl.when(diagonal)
+    def _():
+        pl.semaphore_wait(barrier, 24)
+
+    to_cross(
+        lambda t: cb.at[part_rows(r)], rb.at[x, part_rows(r)], snd.at[0], snd0.at[0], rb_z
+    )
     scatter_rows(0, 1, 3)
 
     @pl.loop(0, ROWS)
@@ -421,12 +446,12 @@
     products_by_columns(0)
     scatter_columns(0)
     sum_start(1, gram_rows(rb, p.at[0]), snd.at[14])
+    scatter_rows_next(0, 1, 3)
+    columns_sum(0)
+    scatter_rows_next(0, 3, 5)
+    wide_z(1)
+    scatter_rows_next(0, 5, 8)
     sum_start(0, gram_rows(rb, rb), snd.at[10])
-    scatter_rows_next(0, 1, 4)
-    wide_z(1)
-    sum_spread(0, sum_middle(0), snd.at[11])
-    scatter_rows_next(0, 4, 8)
-    mat[0] = sum_end(0)
     wide_x(1)
     owned(0)
 
@@ -434,6 +459,7 @@
     rw[x, part_rows(z)] = own[0]
     to_z(lambda t: (own.at[0], rw.at[x, part_rows(z)]), snd.at[12], rw_z)
     forward(rw, z, snd.at[13], rw_x)
+    sum_spread(0, sum_middle(0), snd.at[11])
     wide_r(1, snd.at[15])
 
     def onward(k):
@@ -444,12 +470,16 @@
     chunk = K // 4
     for k, far in enumerate((1, 7, 2, 6, 3, 5, 4)):
         onward(far)
+        if k == 1:
+            mat[0] = sum_end(0)
+        if k in (1, 2):
+            pivots((0,), (k - 1) * K // 2, k * K // 2)
         if k == 3:
             swap_spread(0, cw)
             half = sum_end(1)
             mat[1] = half + half.T
-        part = k % 4 * chunk
-        pivots((k // 4,), part, part + chunk)
+        if k > 3:
+            pivots((1,), (k - 4) * chunk, (k - 3) * chunk)
     columns_here(0, cw)
     split_columns(cw)
     products_by_rows(1)
@@ -467,6 +497,7 @@
         return total + dot_t(part, part)
 
     sum_start(2, lax.fori_loop(0, XS, residual_gram, jnp.zeros((K, K), F32)), snd.at[16])
+    columns_sum(1)
     scatter_rows_next(1, 3, 6)
     sum_spread(2, sum_middle(2), snd.at[17])
     scatter_rows_next(1, 6, 8)
@@ -541,6 +572,8 @@
             vm((2, ROWS, PART, K), F32),
             vm((2, PART, K), F32),
             vm((2, PART, K), F32),
+            vm((2, PART, K), F32),
+            vm((2, PART, K), F32),
             vm((4, K, K), F32),
             vm((4, ROWS, GP, K), F32),
             vm((4, K, K), F32),
@@ -560,6 +593,7 @@
             dma((2, ROWS)),
             dma((2, ROWS)),
             dma((2,)),
+            dma((2,)),
             dma((ZS,)),
             dma((XS,)),
             dma((4, ROWS)),

time: 133 us -> 136 us (1.023)
  Pallas kernels: 129 us -> 132 us
    pallas_call x1, Pallas kernels: 129 us -> 132 us  [per_device(): pl.pallas_call(kernel, out_shape=(jax.ShapeDtypeStruct((SET, K), F32), ja...]
where the time goes in v4:
time: 136 us
  Pallas kernels  132 us (97%)
  local copies, waits for them, and re-layouts  3.44 us (3%)
    pallas_call x1, Pallas kernels, per_device(): pl.pallas_call(kernel, out_shape=(jax.ShapeDtypeStruct((SET, K), F32), ja...  132 us
    unnamed x2, local copies, waits for them, and re-layouts  3.44 us

profile of v4, /device:TPU:1, one launch (start us, length us, event | category | flops | bytes accessed | tf_op | source)
XLA Modules:
  0.0 135.7 jit_solution(7706917660498483188)
XLA Ops:
  0.6 131.6 %block_cg.1 = (f32[640,128]{1,0:T(8,128)}, f32[640,128]{1,0:T(8,128)}) custom-call(f32[12800,128]{1,0:T(8,128)} %bitcast.8, f32[640,128]{1,0:T(8,128)} %bitcast.11), custom_call_target="tpu_custom_call" | custom-call | tf_op jit(solution)/shard_map/block_cg/pallas_call | solution.py:550
  132.3 1.7 %copy.8 = f32[5,1,128,128]{3,2,1,0:T(8,128)} copy(f32[5,1,128,128]{3,2,1,0:T(8,128)} %bitcast.10) | data formatting | bytes 655360
  134.0 1.7 %copy.9 = f32[5,1,128,128]{3,2,1,0:T(8,128)} copy(f32[5,1,128,128]{3,2,1,0:T(8,128)} %bitcast.9) | data formatting | bytes 655360

commit v5 on v3

--- a/solution.py
+++ b/solution.py
@@ -97,11 +97,6 @@
     @pl.when(jnp.logical_not(diagonal))
     def _():
         greet(r, x, r)
-        pl.semaphore_wait(barrier, 25)
-
-    @pl.when(diagonal)
-    def _():
-        pl.semaphore_wait(barrier, 24)
 
     load_b.wait()
 
@@ -300,9 +295,6 @@
 
         sum_spread(k, (gx[k, 0] + gx[k, 1]) + (gx[k, 2] + gx[k, 3]), sem)
 
-    to_cross(
-        lambda t: cb.at[part_rows(r)], rb.at[x, part_rows(r)], snd.at[0], snd0.at[0], rb_z
-    )
     split_columns(cb)
 
     mine = x * ZS + z
@@ -407,6 +399,18 @@
             await_bytes(rows.at[t], rsem.at[t])
 
     products_by_rows(0)
+
+    @pl.when(jnp.logical_not(diagonal))
+    def _():
+        pl.semaphore_wait(barrier, 25)
+
+    @pl.when(diagonal)
+    def _():
+        pl.semaphore_wait(barrier, 24)
+
+    to_cross(
+        lambda t: cb.at[part_rows(r)], rb.at[x, part_rows(r)], snd.at[0], snd0.at[0], rb_z
+    )
     scatter_rows(0, 1, 3)
 
     @pl.loop(0, ROWS)

time: 133 us -> 137 us (1.030)
  Pallas kernels: 129 us -> 133 us
    pallas_call x1, Pallas kernels: 129 us -> 133 us  [per_device(): pl.pallas_call(kernel, out_shape=(jax.ShapeDtypeStruct((SET, K), F32), ja...]
where the time goes in v5:
time: 137 us
  Pallas kernels  133 us (97%)
  local copies, waits for them, and re-layouts  3.44 us (3%)
    pallas_call x1, Pallas kernels, per_device(): pl.pallas_call(kernel, out_shape=(jax.ShapeDtypeStruct((SET, K), F32), ja...  133 us
    unnamed x2, local copies, waits for them, and re-layouts  3.44 us

profile of v5, /device:TPU:1, one launch (start us, length us, event | category | flops | bytes accessed | tf_op | source)
XLA Modules:
  0.0 136.8 jit_solution(4587255516989439658)
XLA Ops:
  0.6 132.8 %block_cg.1 = (f32[640,128]{1,0:T(8,128)}, f32[640,128]{1,0:T(8,128)}) custom-call(f32[12800,128]{1,0:T(8,128)} %bitcast.8, f32[640,128]{1,0:T(8,128)} %bitcast.11), custom_call_target="tpu_custom_call" | custom-call | tf_op jit(solution)/shard_map/block_cg/pallas_call | solution.py:523
  133.4 1.7 %copy.8 = f32[5,1,128,128]{3,2,1,0:T(8,128)} copy(f32[5,1,128,128]{3,2,1,0:T(8,128)} %bitcast.10) | data formatting | bytes 655360
  135.1 1.7 %copy.9 = f32[5,1,128,128]{3,2,1,0:T(8,128)} copy(f32[5,1,128,128]{3,2,1,0:T(8,128)} %bitcast.9) | data formatting | bytes 655360
